TPU v7x, 32 devices: a whole 2x2x4 slice. The times are simulated.
32 devices in a mesh: seq: 8 (over z, y), tp: 4 (over x, core).
Axes of the slice: x: 2, y: 2, z: 4, core: 2. Of those that a mesh axis runs over, the one named last changes fastest.
Arguments:
- tokens: bfloat16 [8192, 1152], P('seq', 'tp'), may hold values from -6 to 6
- out_grad: bfloat16 [8192, 1152], P('seq', 'tp'), may hold values from -6 to 6
- route_mask: int32 [8192], P('seq'), may hold values from 0 to 1, as said below
- kept_counts: int32 [32], replicated, may hold values from 64 to 192, as said below
- labels: int32 [32], replicated, may hold values from 0 to 1000
- timesteps: int32 [32], replicated, may hold values from 0 to 999
- class_table: bfloat16 [1001, 1152], replicated, may hold values from -6 to 6
- ada_weight: bfloat16 [1152, 6, 1152], P(None, None, 'tp'), may hold values from -0.1875 to 0.1875
- ada_bias: bfloat16 [6, 1152], P(None, 'tp'), may hold values from -2 to 2
- qkv_weight: bfloat16 [1152, 3, 1152], P(None, None, 'tp'), may hold values from -0.1875 to 0.1875
- qv_bias: bfloat16 [2, 1152], P(None, 'tp'), may hold values from -2 to 2
- proj_weight: bfloat16 [1152, 1152], P('tp'), may hold values from -0.5 to 0.5
- proj_bias: bfloat16 [1152], P('tp'), may hold values from -2 to 2
- hidden_weight: bfloat16 [1152, 4608], P(None, 'tp'), may hold values from -0.1875 to 0.1875
- hidden_bias: bfloat16 [4608], P('tp'), may hold values from -2 to 2
- output_weight: bfloat16 [4608, 1152], P('tp'), may hold values from -0.09375 to 0.09375
- output_bias: bfloat16 [1152], P('tp'), may hold values from -2 to 2
Outputs:
- output: bfloat16 [8192, 1152], P('seq', 'tp')
- tokens_grad: bfloat16 [8192, 1152], P('seq', 'tp')
- class_grad: float32 [1001, 1152], P(None, 'seq')
- ada_weight_grad: float32 [1152, 6, 1152], P('seq', None, 'tp')
- ada_bias_grad: float32 [6, 1152], P(None, 'tp')
- qkv_weight_grad: float32 [1152, 3, 1152], P('seq', None, 'tp')
- qv_bias_grad: float32 [2, 1152], P(None, 'tp')
- proj_weight_grad: float32 [1152, 1152], P('tp', 'seq')
- proj_bias_grad: float32 [1152], P('tp')
- hidden_weight_grad: float32 [1152, 4608], P('seq', 'tp')
- hidden_bias_grad: float32 [4608], P('tp')
- output_weight_grad: float32 [4608, 1152], P('tp', 'seq')
- output_bias_grad: float32 [1152], P('tp')
Inputs may be any that keep to these rules, and one draw needn't show every extreme that they name: route_mask keeps exactly kept_counts[i] of the 256 tokens of image i. The kept tokens of all images number 512 * 8; the kept tokens of the first j * 4 images exceed j * 512 by 0 to 128 for every j, by exactly 128 for some j, and by 0 at the end. Every aligned block of 4 images has one image with 192 kept tokens. `route_mask`: consistent with kept_counts.
All inputs are finite; a program needn't handle non-finite values.
Results may differ from a plain program's by a relative error of at most 0.025.
The roundings to bfloat16 on the way count: a program that leaves them out, or rounds other values in their place, can miss the bound.
Values may be sent and summed in bfloat16 or wider, within the bound.
A program may use at most 192 MiB of HBM per device.

v0:
```python
import math
import jax
import jax.numpy as jnp
from jax import lax
from jax.sharding import PartitionSpec as P

HEAD_DIM = 72
IMG_DEV = 4
ROWS = 640
NORM_EPS = 1e-06
HIGHEST = lax.Precision.HIGHEST


def exact_dot(left_mat, right_mat):
    return jnp.dot(left_mat, right_mat, precision=HIGHEST, preferred_element_type=jnp.float32)


def time_embed(step_ids, model_width):
    half_width = model_width // 2
    frequency = jnp.exp(-math.log(10000.0) * jnp.arange(half_width, dtype=jnp.float32) / half_width)
    angles = step_ids.astype(jnp.float32)[:, None] * frequency[None, :]
    return jnp.concatenate([jnp.cos(angles), jnp.sin(angles)], axis=1)


def norm_rows(values):
    centered = values - jnp.mean(values, axis=1, keepdims=True)
    inverse = lax.rsqrt(jnp.mean(centered * centered, axis=1, keepdims=True) + NORM_EPS)
    return (centered * inverse, inverse)


def gelu_tanh(values):
    return jax.nn.gelu(values, approximate=True)


def local(
    tokens,
    out_grad,
    route_mask,
    kept_counts,
    labels,
    timesteps,
    class_table,
    ada_weight,
    ada_bias,
    qkv_weight,
    qv_bias,
    proj_weight,
    proj_bias,
    hidden_weight,
    hidden_bias,
    output_weight,
    output_bias,
):
    f32, bf16 = (jnp.float32, jnp.bfloat16)
    seq_index = lax.axis_index("seq")
    tp_index = lax.axis_index("tp")
    seq_size = lax.axis_size("seq")
    col_local = tokens.shape[1]
    model_width = class_table.shape[1]
    head_cols = qkv_weight.shape[2]
    heads_local = head_cols // HEAD_DIM
    slice_width = model_width // seq_size
    images = kept_counts.shape[0]
    scale_factor = HEAD_DIM ** (-0.5)
    col_start = tp_index * col_local
    first_image = seq_index * IMG_DEV
    own_counts = lax.dynamic_slice_in_dim(kept_counts, first_image, IMG_DEV)
    own_ends = jnp.cumsum(own_counts)
    rank = jnp.where(route_mask > 0, jnp.cumsum(route_mask) - 1, -1)
    row_ids = jnp.arange(ROWS, dtype=jnp.int32)
    place = (rank[None, :] == row_ids[:, None]).astype(bf16)
    row_image = jnp.sum((own_ends[None, :] <= row_ids[:, None]).astype(jnp.int32), axis=1)
    row_onehot = (row_image[:, None] == jnp.arange(IMG_DEV, dtype=jnp.int32)[None, :]).astype(f32)

    def whole_rows(part_rows):
        return lax.all_gather(part_rows, "tp", axis=1, tiled=True)

    def column_sum(part_rows):
        return lax.psum_scatter(
            part_rows.astype(bf16), "tp", scatter_dimension=1, tiled=True
        ).astype(f32)

    def own_cols(full_rows):
        return lax.dynamic_slice_in_dim(full_rows, col_start, col_local, 1)

    def reinsert(rows_new, initial):
        placed = jnp.einsum("rt,rc->tc", place, rows_new, preferred_element_type=f32).astype(bf16)
        return jnp.where(route_mask[:, None] > 0, placed, initial)

    label_hot = (
        labels[:, None] == jnp.arange(class_table.shape[0], dtype=jnp.int32)[None, :]
    ).astype(bf16)
    condition = jnp.dot(label_hot, class_table, preferred_element_type=f32) + time_embed(
        timesteps, model_width
    )
    cond_low = jax.nn.silu(condition).astype(bf16)
    cond_own = lax.dynamic_slice_in_dim(cond_low, first_image, IMG_DEV)
    mod_own = (
        jnp.einsum("wd,dcf->wcf", cond_own, ada_weight, preferred_element_type=f32)
        + ada_bias.astype(f32)[None]
    )
    mod_full = lax.all_gather(mod_own, "tp", axis=2, tiled=True)

    def row_full(stretch_id):
        return exact_dot(row_onehot, mod_full[:, stretch_id, :])

    def row_own(stretch_id):
        return exact_dot(row_onehot, mod_own[:, stretch_id, :])

    def input_grads(partial_rows, normed, inverse, scale):
        own_grad = column_sum(partial_rows)
        normed_own = own_cols(normed)
        scaled_grad = own_grad * (1.0 + own_cols(scale))
        mean_grad, mean_cross = lax.psum(
            (
                jnp.sum(scaled_grad, axis=1, keepdims=True) / model_width,
                jnp.sum(scaled_grad * normed_own, axis=1, keepdims=True) / model_width,
            ),
            "tp",
        )
        return (
            own_grad,
            own_grad * normed_own,
            inverse * (scaled_grad - mean_grad - normed_own * mean_cross),
        )

    picked = jnp.dot(place, jnp.concatenate([tokens, out_grad], axis=1), preferred_element_type=f32)
    rows_in = picked[:, :col_local].astype(bf16)
    grad_rows = picked[:, col_local:]
    gate_one = row_own(2)
    gate_two = row_own(5)
    mlp_grad = (grad_rows * gate_two).astype(bf16)
    full_in = whole_rows(rows_in).astype(f32)
    mlp_grad_full = whole_rows(mlp_grad)
    normed_one, inverse_one = norm_rows(full_in)
    scale_one = row_full(1)
    branch_one = (normed_one * (1.0 + scale_one) + row_full(0)).astype(bf16)
    qkv_bias = jnp.stack([qv_bias[0], jnp.zeros_like(qv_bias[0]), qv_bias[1]]).astype(f32)
    qkv_rows = (
        jnp.einsum("rd,dcf->rcf", branch_one, qkv_weight, preferred_element_type=f32)
        + qkv_bias[None]
    ).astype(bf16)
    query_all, key_all, value_all = (
        qkv_rows[:, part].reshape(ROWS, heads_local, HEAD_DIM) for part in range(3)
    )
    same_image = row_image[:, None] == row_image[None, :]
    raw = jnp.einsum("qhe,khe->hqk", query_all, key_all, preferred_element_type=f32) * scale_factor
    masked = jnp.where(same_image[None], raw, -1e30)
    top_score = jnp.max(masked, axis=2, keepdims=True)
    exp_scores = jnp.exp(masked - top_score)
    attn_probs = exp_scores / jnp.sum(exp_scores, axis=2, keepdims=True)
    probs_low = attn_probs.astype(bf16)
    attended = (
        jnp.einsum("hqk,khe->qhe", probs_low, value_all, preferred_element_type=f32)
        .reshape(ROWS, head_cols)
        .astype(bf16)
    )
    attn_out = column_sum(
        jnp.dot(attended, proj_weight, preferred_element_type=f32)
    ) + proj_bias.astype(f32)
    middle = rows_in.astype(f32) + gate_one * attn_out
    middle_full = whole_rows(middle.astype(bf16)).astype(f32)
    normed_two, inverse_two = norm_rows(middle_full)
    scale_two = row_full(4)
    branch_two = (normed_two * (1.0 + scale_two) + row_full(3)).astype(bf16)
    pre_act = jnp.dot(branch_two, hidden_weight, preferred_element_type=f32) + hidden_bias.astype(
        f32
    )
    act_low = gelu_tanh(pre_act).astype(bf16)
    mlp_out = column_sum(
        jnp.dot(act_low, output_weight, preferred_element_type=f32)
    ) + output_bias.astype(f32)
    final_rows = middle + gate_two * mlp_out
    output = reinsert(final_rows.astype(bf16), tokens)
    gate_two_rows = grad_rows * mlp_out
    output_bias_term = jnp.sum(mlp_grad, axis=0, dtype=f32)
    output_weight_term = jnp.einsum(
        "rf,rd->fd", act_low, mlp_grad_full, preferred_element_type=f32
    ).astype(bf16)
    act_grad = jnp.einsum("rd,fd->rf", mlp_grad_full, output_weight, preferred_element_type=f32)
    gelu_pull = jax.vjp(gelu_tanh, pre_act)[1]
    pre_grad = gelu_pull(act_grad)[0].astype(bf16)
    hidden_bias_term = jnp.sum(pre_grad, axis=0, dtype=f32)
    hidden_weight_term = jnp.einsum(
        "rd,rf->df", branch_two, pre_grad, preferred_element_type=f32
    ).astype(bf16)
    two_partial = jnp.einsum("rf,df->rd", pre_grad, hidden_weight, preferred_element_type=f32)
    shift_two_grad, scale_two_grad, two_norm_grad = input_grads(
        two_partial, normed_two, inverse_two, scale_two
    )
    middle_grad = grad_rows + two_norm_grad
    gate_one_rows = middle_grad * attn_out
    attn_grad = (middle_grad * gate_one).astype(bf16)
    proj_bias_term = jnp.sum(attn_grad, axis=0, dtype=f32)
    attn_grad_full = whole_rows(attn_grad)
    proj_weight_term = jnp.einsum(
        "rf,rd->fd", attended, attn_grad_full, preferred_element_type=f32
    ).astype(bf16)
    attended_grad = (
        jnp.einsum("rd,fd->rf", attn_grad_full, proj_weight, preferred_element_type=f32)
        .astype(bf16)
        .reshape(ROWS, heads_local, HEAD_DIM)
    )
    value_term = jnp.einsum("hqk,qhe->khe", probs_low, attended_grad, preferred_element_type=f32)
    prob_grad = jnp.einsum("qhe,khe->hqk", attended_grad, value_all, preferred_element_type=f32)
    row_dot = jnp.sum(attn_probs * prob_grad, axis=2, keepdims=True)
    score_grad = (attn_probs * (prob_grad - row_dot)).astype(bf16)
    query_term = (
        jnp.einsum("hqk,khe->qhe", score_grad, key_all, preferred_element_type=f32) * scale_factor
    )
    key_term = (
        jnp.einsum("hqk,qhe->khe", score_grad, query_all, preferred_element_type=f32) * scale_factor
    )
    qkv_grad = (
        jnp.stack([query_term, key_term, value_term], axis=1)
        .reshape(ROWS, 3, head_cols)
        .astype(bf16)
    )
    qkv_sums = jnp.sum(qkv_grad, axis=0, dtype=f32)
    qkv_weight_term = jnp.einsum(
        "rd,rcf->dcf", branch_one, qkv_grad, preferred_element_type=f32
    ).astype(bf16)
    one_partial = jnp.einsum("rcf,dcf->rd", qkv_grad, qkv_weight, preferred_element_type=f32)
    shift_one_grad, scale_one_grad, one_norm_grad = input_grads(
        one_partial, normed_one, inverse_one, scale_one
    )
    in_grad = middle_grad + one_norm_grad
    tokens_grad = reinsert(in_grad.astype(bf16), out_grad)
    per_row = jnp.concatenate(
        [
            shift_one_grad,
            scale_one_grad,
            gate_one_rows,
            shift_two_grad,
            scale_two_grad,
            gate_two_rows,
        ],
        axis=1,
    )
    mod_grad = jnp.einsum(
        "rw,rf->wf", row_onehot, per_row, precision=HIGHEST, preferred_element_type=f32
    )
    small = jnp.concatenate(
        [
            mod_grad.reshape(-1),
            qkv_sums[0],
            qkv_sums[2],
            proj_bias_term,
            hidden_bias_term,
            output_bias_term,
        ]
    )
    small_all = lax.all_gather(small, "seq", axis=0)
    mod_size = mod_grad.size
    mod_all = small_all[:, :mod_size].reshape(images, 6, col_local)
    bias_sums = jnp.sum(small_all[:, mod_size:], axis=0)
    ada_bias_grad = jnp.sum(mod_all, axis=0)
    qv_bias_grad = bias_sums[: 2 * col_local].reshape(2, col_local)
    at = 2 * col_local
    proj_bias_grad = bias_sums[at : at + col_local]
    at += col_local
    hidden_bias_grad = bias_sums[at : at + hidden_bias.shape[0]]
    at += hidden_bias.shape[0]
    output_bias_grad = bias_sums[at:]
    width_start = seq_index * slice_width
    cond_cols = lax.dynamic_slice_in_dim(condition, width_start, slice_width, 1)
    low_cols = lax.dynamic_slice_in_dim(cond_low, width_start, slice_width, 1)
    ada_weight_grad = jnp.einsum(
        "wd,wcf->dcf", low_cols.astype(f32), mod_all, precision=HIGHEST, preferred_element_type=f32
    )
    ada_rows = lax.dynamic_slice_in_dim(ada_weight, width_start, slice_width, 0)
    cond_grad = lax.psum(
        jnp.einsum(
            "wcf,dcf->wd",
            mod_all,
            ada_rows.astype(f32),
            precision=HIGHEST,
            preferred_element_type=f32,
        ),
        "tp",
    )
    silu_pull = jax.vjp(jax.nn.silu, cond_cols)[1]
    class_grad = jnp.einsum(
        "wc,wd->cd",
        label_hot.astype(f32),
        silu_pull(cond_grad)[0],
        precision=HIGHEST,
        preferred_element_type=f32,
    )
    qkv_weight_grad, proj_weight_grad, hidden_weight_grad, output_weight_grad = (
        lax.psum_scatter(qkv_weight_term, "seq", scatter_dimension=0, tiled=True).astype(f32),
        lax.psum_scatter(proj_weight_term, "seq", scatter_dimension=1, tiled=True).astype(f32),
        lax.psum_scatter(hidden_weight_term, "seq", scatter_dimension=0, tiled=True).astype(f32),
        lax.psum_scatter(output_weight_term, "seq", scatter_dimension=1, tiled=True).astype(f32),
    )
    return (
        output,
        tokens_grad,
        class_grad,
        ada_weight_grad,
        ada_bias_grad,
        qkv_weight_grad,
        qv_bias_grad,
        proj_weight_grad,
        proj_bias_grad,
        hidden_weight_grad,
        hidden_bias_grad,
        output_weight_grad,
        output_bias_grad,
    )


def solution(mesh):
    return jax.shard_map(
        local,
        mesh=mesh,
        in_specs=(
            P("seq", "tp"),
            P("seq", "tp"),
            P("seq"),
            P(),
            P(),
            P(),
            P(),
            P(None, None, "tp"),
            P(None, "tp"),
            P(None, None, "tp"),
            P(None, "tp"),
            P("tp", None),
            P("tp"),
            P(None, "tp"),
            P("tp"),
            P("tp", None),
            P("tp"),
        ),
        out_specs=(
            P("seq", "tp"),
            P("seq", "tp"),
            P(None, "seq"),
            P("seq", None, "tp"),
            P(None, "tp"),
            P("seq", None, "tp"),
            P(None, "tp"),
            P("tp", "seq"),
            P("tp"),
            P("seq", "tp"),
            P("tp"),
            P("tp", "seq"),
            P("tp"),
        ),
        check_vma=False,
    )
```

profile of v0, /device:TPU:0, one launch (start us, length us, event | category | flops | bytes accessed | tf_op | source)
XLA Modules:
  0.0 589.2 jit_solution(4795627765267242598)
XLA Ops:
  17.3 3.5 convolution_add_fusion.4
  21.1 26.5 %all_gather.22 = f32[4,6,1152]{1,0,2:T(4,128)S(1)} all-gather(f32[4,6,288]{1,0,2:T(4,128)S(1)} %copy.102), channel_id=1, replica_groups=mesh['seq'=8,'tp'=4] {'tp'}, dimensions={2}, use_global_device_ids=true | all-gather | bytes 138240 | tf_op jit(solution)/shard_map/all_gather | solution.py:102
  47.6 6.0 %fusion.109 = (f32[4,1,1152]{1,0,2:T(4,128)}, f32[4,1,1152]{1,0,2:T(4,128)}, f32[4,1,1152]{1,0,2:T(4,128)}, f32[4,1,1152]{1,0,2:T(4,128)}) fusion(f32[4,6,1152]{1,0,2:T(4,128)S(1)} %all_gather.22), kind=kLoop, calls=%fused_computation.184 | loop fusion | bytes 147456 | tf_op jit(solution)/shard_map/slice | solution.py:105
  66.1 3.9 fusion.21
  72.7 6.5 %fusion.113 = (f32[4,640]{1,0:T(4,128)S(1)}, f32[4,640,640]{1,2,0:T(8,128)}) fusion(pred[640,640]{0,1:T(8,128)(4,1)} %broadcast_compare_fusion, bf16[640,4,72]{0,2,1:T(8,128)(2,1)S(1)} %bitcast.99, bf16[640,4,72]{0,2,1:T(8,128)(2,1)S(1)} %bitcast.97), kind=kOutput, calls=%fused_computation.188 | convolution fusion | flops 242483840 | bytes 7710720 | tf_op jit(solution)/shard_map/sub | solution.py:150
  79.2 3.7 fusion.38
  88.8 25.1 %reduce-scatter.9.cloned.1.call-done = bf16[640,288]{0,1:T(8,128)(2,1)} async-done(((bf16[640,1152]{0,1:T(8,128)(2,1)}), bf16[640,288]{0,1:T(8,128)(2,1)}) %reduce-scatter.9.cloned.1.call-update) | async-done | bytes 368656 | tf_op jit(solution)/shard_map/reduce_scatter | solution.py:79
  124.4 10.8 %all-gather.10.cloned.1.call-done = bf16[640,1152]{0,1:T(8,128)(2,1)} async-done(((bf16[640,288]{0,1:T(8,128)(2,1)}), bf16[640,1152]{0,1:T(8,128)(2,1)}) %all-gather.10.cloned.1.call-update) | async-done | bytes 1474576 | tf_op jit(solution)/shard_map/all_gather | solution.py:76
  135.2 6.1 %fusion.115 = f32[640,1152]{0,1:T(8,128)} fusion(bf16[1152,1152]{1,0:T(8,128)(2,1)} %param.32, bf16[640,1152]{0,1:T(8,128)(2,1)} %all-gather.10.cloned.1.call-done), kind=kOutput, calls=%fused_computation.190 | convolution fusion | flops 1698693120 | bytes 7077888 | tf_op jit(solution)/shard_map/rd,fd->rf/dot_general | solution.py:180
  141.3 15.1 %all-gather.8.cloned.1.call-done = bf16[640,1152]{0,1:T(8,128)(2,1)} async-done(((bf16[640,288]{0,1:T(8,128)(2,1)}), bf16[640,1152]{0,1:T(8,128)(2,1)}) %all-gather.8.cloned.1.call-update) | async-done | bytes 1474576 | tf_op jit(solution)/shard_map/all_gather | solution.py:76
  160.0 3.9 fusion.11
  164.0 6.0 %convert_reduce_fusion.2 = (f32[1152]{0:T(1024)S(1)}, bf16[640,1152]{0,1:T(8,128)(2,1)S(1)}, f32[640,1152]{0,1:T(8,128)}) fusion(f32[640,1152]{0,1:T(8,128)S(1)} %copy-done.43, f32[1152]{0:T(1024)S(1)} %convert_element_type.178, bf16[640,1152]{0,1:T(8,128)(2,1)S(1)} %fusion.11, bf16[1152,1152]{1,0:T(8,128)(2,1)S(1)} %copy-done), kind=kOutput, calls=%fused_computation.42 | convolution fusion | flops 1715649408 | bytes 11510784 | tf_op jit(solution)/shard_map/dot_general | solution.py:166
  171.2 4.0 convolution_convert_fusion.3
  175.2 3.4 fusion.4
  178.6 24.3 %reduce-scatter.13.cloned.1.call-done = bf16[640,288]{0,1:T(8,128)(2,1)} async-done(((bf16[640,1152]{0,1:T(8,128)(2,1)}), bf16[640,288]{0,1:T(8,128)(2,1)}) %reduce-scatter.13.cloned.1.call-update) | async-done | bytes 368656 | tf_op jit(solution)/shard_map/reduce_scatter | solution.py:79
  204.3 5.9 all-reduce.1
  213.2 6.6 %convolution_convert_fusion.4 = bf16[640,1152]{0,1:T(8,128)(2,1)} fusion(bf16[1152,1152]{1,0:T(8,128)(2,1)} %param.32, f32[640,1152]{0,1:T(8,128)} %get-tuple-element.54), kind=kOutput, calls=%fused_computation.28 | convolution fusion | flops 1706065920 | bytes 7077888 | tf_op jit(solution)/shard_map/dot_general | solution.py:171
  219.8 5.4 convolution_convert_fusion.1
  225.3 5.8 convolution_convert_fusion
  237.9 4.1 multiply_reduce_fusion
  247.9 4.3 fusion.41
  252.2 3.2 fusion.9
  257.7 5.6 convolution_convert_fusion.2
  263.7 3.2 fusion.35
  267.2 71.5 %reduce-scatter.21.cloned.1.call-done = bf16[144,1152]{1,0:T(8,128)(2,1)} async-done(((bf16[1152,1152]{1,0:T(8,128)(2,1)}), bf16[144,1152]{1,0:T(8,128)(2,1)}) %reduce-scatter.21.cloned.1.call-update) | async-done | bytes 331792 | tf_op jit(solution)/shard_map/reduce_scatter | solution.py:293
  340.5 71.4 %reduce-scatter.23.cloned.1.call-done = bf16[1152,144]{0,1:T(8,128)(2,1)} async-done(((bf16[1152,1152]{0,1:T(8,128)(2,1)}), bf16[1152,144]{0,1:T(8,128)(2,1)}) %reduce-scatter.23.cloned.1.call-update) | async-done | bytes 331792 | tf_op jit(solution)/shard_map/reduce_scatter | solution.py:294
  413.8 62.3 %reduce-scatter.19.cloned.1.call-done = bf16[288,144]{0,1:T(8,128)(2,1)} async-done(((bf16[288,1152]{0,1:T(8,128)(2,1)}), bf16[288,144]{0,1:T(8,128)(2,1)}) %reduce-scatter.19.cloned.1.call-update) | async-done | bytes 82960 | tf_op jit(solution)/shard_map/reduce_scatter | solution.py:292
  477.7 27.7 %reduce-scatter.15.cloned.1.call-done = bf16[640,288]{0,1:T(8,128)(2,1)} async-done(((bf16[640,1152]{0,1:T(8,128)(2,1)}), bf16[640,288]{0,1:T(8,128)(2,1)}) %reduce-scatter.15.cloned.1.call-update) | async-done | bytes 368656 | tf_op jit(solution)/shard_map/reduce_scatter | solution.py:79
  512.1 31.6 %all-gather = f32[73728]{0:T(1024)S(1)} all-gather(f32[9216]{0:T(1024)S(1)} %concatenate.21), channel_id=2, replica_groups=mesh['seq'=8,'tp'=4] {'seq'}, dimensions={0}, use_global_device_ids=true | all-gather | bytes 331776 | tf_op jit(solution)/shard_map/all_gather | solution.py:253
  548.1 11.1 %all-reduce = (f32[640]{0:T(1024)S(1)}, f32[640]{0:T(1024)S(1)}, f32[32,144]{1,0:T(8,128)S(1)}) all-reduce(f32[640]{0:T(1024)S(1)} %broadcast_multiply_fusion, f32[640]{0:T(1024)S(1)} %broadcast_multiply_fusion.1, f32[32,144]{1,0:T(8,128)S(1)} %convolution_bitcast_fusion.1), channel_id=1, replica_groups=mesh['seq'=8,'tp'=4] {'tp'}, use_global_device_ids=true, to_apply=%region_22.23 | all-reduce | flops 5888 | bytes 47104 | tf_op jit(solution)/shard_map/psum | solution.py:114
  563.9 3.5 fusion.34
  567.3 12.9 %reduce-scatter.17.cloned.1.call-done = bf16[144,3,288]{2,0,1:T(8,128)(2,1)} async-done(((bf16[1152,3,288]{2,0,1:T(8,128)(2,1)}), bf16[144,3,288]{2,0,1:T(8,128)(2,1)}) %reduce-scatter.17.cloned.1.call-update) | async-done | bytes 248848 | tf_op jit(solution)/shard_map/reduce_scatter | solution.py:291
  (202 shorter events, 89.4 us)
Async XLA Ops:
  7.2 156.8 %copy-start = (bf16[1152,1152]{1,0:T(8,128)(2,1)S(1)}, bf16[1152,1152]{1,0:T(8,128)(2,1)}, u32[]{:S(2)}) copy-start(bf16[1152,1152]{1,0:T(8,128)(2,1)} %param.30) | copy-start | bytes 7962628
  7.2 55.3 %all-gather.6.cloned.1.call-start = ((), (), s32[]{:S(2)}) async-start(), calls=%async_computation.8 | async-start | bytes 1843200 | tf_op jit(solution)/shard_map/all_gather | solution.py:76
  9.3 5.1 copy-start.29
  13.7 100.2 %reduce-scatter.9.cloned.1.call-start = ((), (), s32[]{:S(2)}) async-start(), calls=%async_computation.9 | async-start | bytes 1843200 | tf_op jit(solution)/shard_map/reduce_scatter | solution.py:79
  72.7 6.5 %copy-start.16 = (bf16[640,1,288]{0,2,1:T(8,128)(2,1)}, bf16[640,1,288]{0,2,1:T(8,128)(2,1)S(1)}, u32[]{:S(2)}) copy-start(bf16[640,1,288]{0,2,1:T(8,128)(2,1)S(1)} %get-tuple-element.38) | copy-start | bytes 1105924
  72.7 6.5 %copy-start.17 = (bf16[640,1,288]{0,2,1:T(8,128)(2,1)}, bf16[640,1,288]{0,2,1:T(8,128)(2,1)S(1)}, u32[]{:S(2)}) copy-start(bf16[640,1,288]{0,2,1:T(8,128)(2,1)S(1)} %get-tuple-element.39) | copy-start | bytes 1105924
  83.7 5.1 copy-start.30
  85.9 31.0 %copy-start.28 = (bf16[1152]{0:T(1024)(128)(2,1)S(1)}, bf16[1152]{0:T(1024)(128)(2,1)}, u32[]{:S(2)}) copy-start(bf16[1152]{0:T(1024)(128)(2,1)} %param.31) | copy-start | bytes 6916
  85.9 49.3 %all-gather.10.cloned.1.call-start = ((), (), s32[]{:S(2)}) async-start(), calls=%async_computation.12 | async-start | bytes 1843200 | tf_op jit(solution)/shard_map/all_gather | solution.py:76
  88.7 67.7 %all-gather.8.cloned.1.call-start = ((), (), s32[]{:S(2)}) async-start(), calls=%async_computation.10 | async-start | bytes 1843200 | tf_op jit(solution)/shard_map/all_gather | solution.py:76
  116.8 86.1 %reduce-scatter.13.cloned.1.call-start = ((), (), s32[]{:S(2)}) async-start(), calls=%async_computation.13 | async-start | bytes 1843200 | tf_op jit(solution)/shard_map/reduce_scatter | solution.py:79
  164.0 6.0 %copy-start.12 = (bf16[640,1152]{0,1:T(8,128)(2,1)}, bf16[640,1152]{0,1:T(8,128)(2,1)S(1)}, u32[]{:S(2)}) copy-start(bf16[640,1152]{0,1:T(8,128)(2,1)S(1)} %fusion.11) | copy-start | bytes 4423684
  175.2 27.7 %copy-start.5 = (f32[640,1152]{0,1:T(8,128)S(1)}, f32[640,1152]{0,1:T(8,128)}, u32[]{:S(2)}) copy-start(f32[640,1152]{0,1:T(8,128)} %fusion.57) | copy-start | bytes 8847364
  175.2 58.3 %all-gather.12.cloned.1.call-start = ((), (), s32[]{:S(2)}) async-start(), calls=%async_computation.14 | async-start | bytes 1843200 | tf_op jit(solution)/shard_map/all_gather | solution.py:76
  213.1 50.6 %reduce-scatter.11.cloned.1.call-start = ((), (), s32[]{:S(2)}) async-start(), calls=%async_computation.11 | async-start | bytes 1843200 | tf_op jit(solution)/shard_map/reduce_scatter | solution.py:79
  213.2 6.7 %copy-start.13 = (bf16[640,1152]{0,1:T(8,128)(2,1)S(1)}, bf16[640,1152]{0,1:T(8,128)(2,1)}, u32[]{:S(2)}) copy-start(bf16[640,1152]{0,1:T(8,128)(2,1)} %copy-done.12) | copy-start | bytes 4423684
  219.8 5.6 copy-start.34
  219.8 118.9 %reduce-scatter.21.cloned.1.call-start = ((), (), s32[]{:S(2)}) async-start(), calls=%async_computation.18 | async-start | bytes 2985984 | tf_op jit(solution)/shard_map/reduce_scatter | solution.py:293
  225.3 186.7 %reduce-scatter.23.cloned.1.call-start = ((), (), s32[]{:S(2)}) async-start(), calls=%async_computation.19 | async-start | bytes 2985984 | tf_op jit(solution)/shard_map/reduce_scatter | solution.py:294
  231.2 4.7 copy-start.40
  231.2 244.9 %reduce-scatter.19.cloned.1.call-start = ((), (), s32[]{:S(2)}) async-start(), calls=%async_computation.17 | async-start | bytes 995328 | tf_op jit(solution)/shard_map/reduce_scatter | solution.py:292
  235.9 6.1 %copy-start.41 = (bf16[640,288]{0,1:T(8,128)(2,1)}, bf16[640,288]{0,1:T(8,128)(2,1)S(1)}, u32[]{:S(2)}) copy-start(bf16[640,288]{0,1:T(8,128)(2,1)S(1)} %convolution_convert_fusion.7) | copy-start | bytes 1105924
  237.9 5.1 slice-start.1
  246.0 259.4 %reduce-scatter.15.cloned.1.call-start = ((), (), s32[]{:S(2)}) async-start(), calls=%async_computation.15 | async-start | bytes 1843200 | tf_op jit(solution)/shard_map/reduce_scatter | solution.py:79
  255.5 324.8 %reduce-scatter.17.cloned.1.call-start = ((), (), s32[]{:S(2)}) async-start(), calls=%async_computation.16 | async-start | bytes 2985984 | tf_op jit(solution)/shard_map/reduce_scatter | solution.py:291
  257.7 6.0 %copy-start.7 = (f32[640,576]{0,1:T(8,128)S(1)}, f32[640,576]{0,1:T(8,128)}, u32[]{:S(2)}) copy-start(f32[640,576]{0,1:T(8,128)} %copy-done.6) | copy-start | bytes 4423684
  257.7 6.0 %copy-start.10 = (f32[640,288]{0,1:T(8,128)S(1)}, f32[640,288]{0,1:T(8,128)}, u32[]{:S(2)}) copy-start(f32[640,288]{0,1:T(8,128)} %get-tuple-element.52) | copy-start | bytes 2211844
  257.7 6.0 %copy-start.14 = (bf16[640,288]{0,1:T(8,128)(2,1)S(1)}, bf16[640,288]{0,1:T(8,128)(2,1)}, u32[]{:S(2)}) copy-start(bf16[640,288]{0,1:T(8,128)(2,1)} %reduce-scatter.9.cloned.1.call-done) | copy-start | bytes 1105924
  267.2 240.9 %copy-start.9 = (f32[640,288]{0,1:T(8,128)S(1)}, f32[640,288]{0,1:T(8,128)}, u32[]{:S(2)}) copy-start(f32[640,288]{0,1:T(8,128)} %get-tuple-element.30) | copy-start | bytes 2211844
  413.8 94.4 %copy-start.8 = (bf16[640,288]{0,1:T(8,128)(2,1)S(1)}, bf16[640,288]{0,1:T(8,128)(2,1)}, u32[]{:S(2)}) copy-start(bf16[640,288]{0,1:T(8,128)(2,1)} %reduce-scatter.13.cloned.1.call-done) | copy-start | bytes 1105924
  543.7 20.1 %copy-start.15 = (bf16[640,288]{0,1:T(8,128)(2,1)S(1)}, bf16[640,288]{0,1:T(8,128)(2,1)}, u32[]{:S(2)}) copy-start(bf16[640,288]{0,1:T(8,128)(2,1)} %reduce-scatter.15.cloned.1.call-done) | copy-start | bytes 1105924
  562.0 20.1 %copy-start.1 = (bf16[1152,1152]{1,0:T(8,128)(2,1)S(1)}, bf16[1152,1152]{1,0:T(8,128)(2,1)}, u32[]{:S(2)}) copy-start(bf16[1152,1152]{1,0:T(8,128)(2,1)} %param.30) | copy-start | bytes 7962628
  (27 other events, 84.6 us)
Sparse Core Ops, SparseCore 0:
  13.8 29.6 all-gather.5
  86.0 27.8 reduce-scatter.8
  116.1 19.0 all-gather.9
  137.3 19.0 all-gather.7
  175.3 27.5 reduce-scatter.12
  213.2 20.2 all-gather.11
  236.1 27.5 reduce-scatter.10
  267.8 70.8 reduce-scatter.20
  342.4 69.5 reduce-scatter.22
  416.2 59.8 reduce-scatter.18
  478.9 26.4 reduce-scatter.14
  508.9 71.3 reduce-scatter.16
where the time goes:
time: 595 us; the launch traced here: 589 us
  waiting for transfers between devices  324 us (54%)
  matrix products  117 us (20%)
  blocking collectives  75 us (13%)
  other arithmetic  33.7 us (6%)
  local copies, waits for them, and re-layouts  23.8 us (4%)
  between operations  15.1 us (3%)
    reduce_scatter x4, waiting for transfers between devices, column_sum(): lax.psum_scatter(part_rows.astype(bf16), 'tp', scatter_dimension=1, tiled...  77.5 us
    reduce_scatter x1, waiting for transfers between devices, local(): lax.psum_scatter(hidden_weight_term, 'seq', scatter_dimension=0, tiled=True)  71.5 us
    reduce_scatter x1, waiting for transfers between devices, local(): lax.psum_scatter(output_weight_term, 'seq', scatter_dimension=1, tiled=True)  71.4 us
    reduce_scatter x1, waiting for transfers between devices, local(): lax.psum_scatter(proj_weight_term, 'seq', scatter_dimension=1, tiled=True)  62.3 us
    all_gather x1, blocking collectives, local(): small_all = lax.all_gather(small, 'seq', axis=0)  31.6 us
    all_gather x4, waiting for transfers between devices, whole_rows(): return lax.all_gather(part_rows, 'tp', axis=1, tiled=True)  28 us
    all_gather x1, blocking collectives, local(): mod_full = lax.all_gather(mod_own, 'tp', axis=2, tiled=True)  26.5 us
    dot_general x6, matrix products, exact_dot(): jnp.dot(left_mat, right_mat, precision=HIGHEST, preferred_element_type=jn...  19.7 us
  transfers between devices with their start and end apart: 12, of which 11 were waited for; matrix products, arithmetic and copies ran while one was open for 20% of the time, Pallas kernels for 0%

commit v1 on v0

--- a/solution.py
+++ b/solution.py
@@ -9,6 +9,29 @@
 ROWS = 640
 NORM_EPS = 1e-06
 HIGHEST = lax.Precision.HIGHEST
+
+
+def get_vector(obj, device_axis):
+    later, w_next, mid_arr = (
+        jax.lax.axis_size(device_axis),
+        jax.lax.axis_index(device_axis),
+        obj.shape[2],
+    )
+    state_next, prior = (obj, 1)
+    while prior < later:
+        state_next = jnp.concatenate(
+            [
+                state_next,
+                jax.lax.ppermute(
+                    state_next,
+                    axis_name=device_axis,
+                    perm=[(pp, (pp - prior) % later) for pp in range(later)],
+                ),
+            ],
+            2,
+        )
+        prior = 2 * prior
+    return jnp.roll(state_next, w_next * mid_arr, 2)
 
 
 def exact_dot(left_mat, right_mat):
@@ -99,7 +122,7 @@
         jnp.einsum("wd,dcf->wcf", cond_own, ada_weight, preferred_element_type=f32)
         + ada_bias.astype(f32)[None]
     )
-    mod_full = lax.all_gather(mod_own, "tp", axis=2, tiled=True)
+    mod_full = get_vector(mod_own, "tp")
 
     def row_full(stretch_id):
         return exact_dot(row_onehot, mod_full[:, stretch_id, :])

time: 595 us -> 569 us (0.956)
  blocking collectives: 75 us -> 48.6 us
  local copies, waits for them, and re-layouts: 23.8 us -> 8.91 us
  waiting for transfers between devices: 324 us -> 337 us
    all_gather x1 -> x0, blocking collectives: 26.5 us -> none  [local(): mod_full = lax.all_gather(mod_own, 'tp', axis=2, tiled=True)]
    slice x6 -> x1, local copies, waits for them, and re-layouts: 15 us -> 0.07 us  [the longest x5 14.9 us: row_full(): return exact_dot(row_onehot, mod_full[:, stretch_id, :])]
    ppermute x0 -> x2, waiting for transfers between devices: none -> 6.76 us  [get_vector(): jax.lax.ppermute(state_next, axis_name=device_axis, perm=[(pp, (pp - prio...]
  transfers between devices with their start and end apart: 12 -> 14, of which waited for: 11 -> 14; matrix products, arithmetic and copies ran while one was open for 20% -> 19% of each run, Pallas kernels for 0% -> 0%
where the time goes in v1:
time: 569 us; the launch traced here: 565 us
  waiting for transfers between devices  337 us (59%)
  matrix products  118 us (21%)
  blocking collectives  48.6 us (9%)
  other arithmetic  33.8 us (6%)
  between operations  15.1 us (3%)
  local copies, waits for them, and re-layouts  8.91 us (2%)
    reduce_scatter x4, waiting for transfers between devices, column_sum(): lax.psum_scatter(part_rows.astype(bf16), 'tp', scatter_dimension=1, tiled...  77.6 us
    reduce_scatter x1, waiting for transfers between devices, local(): lax.psum_scatter(output_weight_term, 'seq', scatter_dimension=1, tiled=True)  71.7 us
    reduce_scatter x1, waiting for transfers between devices, local(): lax.psum_scatter(hidden_weight_term, 'seq', scatter_dimension=0, tiled=True)  71.7 us
    reduce_scatter x1, waiting for transfers between devices, local(): lax.psum_scatter(proj_weight_term, 'seq', scatter_dimension=1, tiled=True)  62.5 us
    all_gather x4, waiting for transfers between devices, whole_rows(): return lax.all_gather(part_rows, 'tp', axis=1, tiled=True)  33.4 us
    all_gather x1, blocking collectives, local(): small_all = lax.all_gather(small, 'seq', axis=0)  31.7 us
    dot_general x6, matrix products, exact_dot(): jnp.dot(left_mat, right_mat, precision=HIGHEST, preferred_element_type=jn...  20.8 us
    psum x2, blocking collectives, input_grads(): lax.psum((jnp.sum(scaled_grad, axis=1, keepdims=True) / model_width, jnp....  16.8 us
  transfers between devices with their start and end apart: 14, of which 14 were waited for; matrix products, arithmetic and copies ran while one was open for 19% of the time, Pallas kernels for 0%

profile of v1, /device:TPU:0, one launch (start us, length us, event | category | flops | bytes accessed | tf_op | source)
XLA Modules:
  0.0 565.0 jit_solution(3516583838540602221)
XLA Ops:
  17.1 3.5 convolution_add_fusion.4
  25.5 6.1 %collective-permute-done.1 = f32[4,6,576]{2,0,1:T(4,128)S(1)} collective-permute-done((f32[4,6,576]{2,0,1:T(4,128)S(1)}, f32[4,6,576]{2,0,1:T(4,128)S(1)}, u32[]{:S(2)}, u32[]{:S(2)}) %collective-permute-start.1) | collective-permute-done | bytes 55328 | tf_op jit(solution)/shard_map/ppermute | solution.py:25
  31.9 3.2 fusion.59
  40.6 4.0 fusion.21
  47.4 6.5 %fusion.112 = (f32[4,640]{1,0:T(4,128)S(1)}, f32[4,640,640]{1,2,0:T(8,128)}) fusion(pred[640,640]{0,1:T(8,128)(4,1)} %broadcast_compare_fusion, bf16[640,4,72]{0,2,1:T(8,128)(2,1)S(1)} %bitcast.99, bf16[640,4,72]{0,2,1:T(8,128)(2,1)S(1)} %bitcast.97), kind=kOutput, calls=%fused_computation.192 | convolution fusion | flops 242483840 | bytes 7710720 | tf_op jit(solution)/shard_map/sub | solution.py:173
  53.8 3.7 fusion.38
  63.4 25.2 %reduce-scatter.9.cloned.1.call-done = bf16[640,288]{0,1:T(8,128)(2,1)} async-done(((bf16[640,1152]{0,1:T(8,128)(2,1)}), bf16[640,288]{0,1:T(8,128)(2,1)}) %reduce-scatter.9.cloned.1.call-update) | async-done | bytes 368656 | tf_op jit(solution)/shard_map/reduce_scatter | solution.py:102
  91.8 3.9 fusion.57
  95.7 14.3 %all-gather.10.cloned.1.call-done = bf16[640,1152]{0,1:T(8,128)(2,1)} async-done(((bf16[640,288]{0,1:T(8,128)(2,1)}), bf16[640,1152]{0,1:T(8,128)(2,1)}) %all-gather.10.cloned.1.call-update) | async-done | bytes 1474576 | tf_op jit(solution)/shard_map/all_gather | solution.py:99
  110.0 6.1 %fusion.114 = f32[640,1152]{0,1:T(8,128)} fusion(bf16[1152,1152]{1,0:T(8,128)(2,1)} %param.32, bf16[640,1152]{0,1:T(8,128)(2,1)} %all-gather.10.cloned.1.call-done), kind=kOutput, calls=%fused_computation.194 | convolution fusion | flops 1698693120 | bytes 7077888 | tf_op jit(solution)/shard_map/rd,fd->rf/dot_general | solution.py:203
  116.1 15.1 %all-gather.8.cloned.1.call-done = bf16[640,1152]{0,1:T(8,128)(2,1)} async-done(((bf16[640,288]{0,1:T(8,128)(2,1)}), bf16[640,1152]{0,1:T(8,128)(2,1)}) %all-gather.8.cloned.1.call-update) | async-done | bytes 1474576 | tf_op jit(solution)/shard_map/all_gather | solution.py:99
  134.8 4.0 fusion.11
  138.9 6.0 %convert_reduce_fusion.2 = (f32[1152]{0:T(1024)S(1)}, bf16[640,1152]{0,1:T(8,128)(2,1)S(1)}, f32[640,1152]{0,1:T(8,128)}) fusion(f32[640,1152]{0,1:T(8,128)S(1)} %copy-done.44, f32[1152]{0:T(1024)S(1)} %convert_element_type.178, bf16[640,1152]{0,1:T(8,128)(2,1)S(1)} %fusion.11, bf16[1152,1152]{1,0:T(8,128)(2,1)S(1)} %copy-done), kind=kOutput, calls=%fused_computation.42 | convolution fusion | flops 1715649408 | bytes 11510784 | tf_op jit(solution)/shard_map/dot_general | solution.py:189
  146.1 3.9 convolution_convert_fusion.3
  150.1 3.4 fusion.4
  153.5 24.3 %reduce-scatter.13.cloned.1.call-done = bf16[640,288]{0,1:T(8,128)(2,1)} async-done(((bf16[640,1152]{0,1:T(8,128)(2,1)}), bf16[640,288]{0,1:T(8,128)(2,1)}) %reduce-scatter.13.cloned.1.call-update) | async-done | bytes 368656 | tf_op jit(solution)/shard_map/reduce_scatter | solution.py:102
  179.1 5.9 %all-reduce.1 = (f32[640]{0:T(1024)S(1)}, f32[640]{0:T(1024)S(1)}) all-reduce(f32[640]{0:T(1024)S(1)} %get-tuple-element.53, f32[640]{0:T(1024)S(1)} %get-tuple-element.54), channel_id=1, replica_groups=mesh['seq'=8,'tp'=4] {'tp'}, use_global_device_ids=true, to_apply=%region_16.17 | all-reduce | flops 1280 | bytes 10240 | tf_op jit(solution)/shard_map/psum | solution.py:137
  188.0 6.5 %convolution_convert_fusion.4 = bf16[640,1152]{0,1:T(8,128)(2,1)} fusion(bf16[1152,1152]{1,0:T(8,128)(2,1)} %param.32, f32[640,1152]{0,1:T(8,128)} %get-tuple-element.50), kind=kOutput, calls=%fused_computation.28 | convolution fusion | flops 1706065920 | bytes 7077888 | tf_op jit(solution)/shard_map/dot_general | solution.py:194
  194.6 5.4 convolution_convert_fusion.1
  200.2 5.8 %convolution_convert_fusion = bf16[1152,1152]{0,1:T(8,128)(2,1)} fusion(bf16[640,1152]{0,1:T(8,128)(2,1)S(1)} %copy-done.35, f32[640,1152]{0,1:T(8,128)} %get-tuple-element.50), kind=kOutput, calls=%fused_computation.1 | convolution fusion | flops 1706655744 | bytes 7077888 | tf_op jit(solution)/shard_map/rf,rd->fd/dot_general | solution.py:200
  212.7 4.1 multiply_reduce_fusion
  222.7 4.3 fusion.41
  227.1 3.2 fusion.9
  232.5 5.5 convolution_convert_fusion.2
  242.0 71.7 %reduce-scatter.21.cloned.1.call-done = bf16[144,1152]{1,0:T(8,128)(2,1)} async-done(((bf16[1152,1152]{1,0:T(8,128)(2,1)}), bf16[144,1152]{1,0:T(8,128)(2,1)}) %reduce-scatter.21.cloned.1.call-update) | async-done | bytes 331792 | tf_op jit(solution)/shard_map/reduce_scatter | solution.py:316
  315.5 71.7 %reduce-scatter.23.cloned.1.call-done = bf16[1152,144]{0,1:T(8,128)(2,1)} async-done(((bf16[1152,1152]{0,1:T(8,128)(2,1)}), bf16[1152,144]{0,1:T(8,128)(2,1)}) %reduce-scatter.23.cloned.1.call-update) | async-done | bytes 331792 | tf_op jit(solution)/shard_map/reduce_scatter | solution.py:317
  389.1 62.5 %reduce-scatter.19.cloned.1.call-done = bf16[288,144]{0,1:T(8,128)(2,1)} async-done(((bf16[288,1152]{0,1:T(8,128)(2,1)}), bf16[288,144]{0,1:T(8,128)(2,1)}) %reduce-scatter.19.cloned.1.call-update) | async-done | bytes 82960 | tf_op jit(solution)/shard_map/reduce_scatter | solution.py:315
  453.2 27.7 %reduce-scatter.15.cloned.1.call-done = bf16[640,288]{0,1:T(8,128)(2,1)} async-done(((bf16[640,1152]{0,1:T(8,128)(2,1)}), bf16[640,288]{0,1:T(8,128)(2,1)}) %reduce-scatter.15.cloned.1.call-update) | async-done | bytes 368656 | tf_op jit(solution)/shard_map/reduce_scatter | solution.py:102
  487.6 31.7 %all-gather = f32[73728]{0:T(1024)S(1)} all-gather(f32[9216]{0:T(1024)S(1)} %concatenate.33), channel_id=2, replica_groups=mesh['seq'=8,'tp'=4] {'seq'}, dimensions={0}, use_global_device_ids=true | all-gather | bytes 331776 | tf_op jit(solution)/shard_map/all_gather | solution.py:276
  523.7 11.0 %all-reduce = (f32[640]{0:T(1024)S(1)}, f32[640]{0:T(1024)S(1)}, f32[32,144]{1,0:T(8,128)S(1)}) all-reduce(f32[640]{0:T(1024)S(1)} %broadcast_multiply_fusion, f32[640]{0:T(1024)S(1)} %broadcast_multiply_fusion.1, f32[32,144]{1,0:T(8,128)S(1)} %convolution_bitcast_fusion.1), channel_id=1, replica_groups=mesh['seq'=8,'tp'=4] {'tp'}, use_global_device_ids=true, to_apply=%region_22.23 | all-reduce | flops 5888 | bytes 47104 | tf_op jit(solution)/shard_map/psum | solution.py:137
  539.3 3.5 fusion.34
  542.8 13.2 %reduce-scatter.17.cloned.1.call-done = bf16[144,3,288]{2,0,1:T(8,128)(2,1)} async-done(((bf16[1152,3,288]{2,0,1:T(8,128)(2,1)}), bf16[144,3,288]{2,0,1:T(8,128)(2,1)}) %reduce-scatter.17.cloned.1.call-update) | async-done | bytes 248848 | tf_op jit(solution)/shard_map/reduce_scatter | solution.py:314
  (203 shorter events, 83.0 us)
Async XLA Ops:
  7.2 131.7 %copy-start = (bf16[1152,1152]{1,0:T(8,128)(2,1)S(1)}, bf16[1152,1152]{1,0:T(8,128)(2,1)}, u32[]{:S(2)}) copy-start(bf16[1152,1152]{1,0:T(8,128)(2,1)} %param.30) | copy-start | bytes 7962628
  7.2 29.8 %all-gather.6.cloned.1.call-start = ((), (), s32[]{:S(2)}) async-start(), calls=%async_computation.8 | async-start | bytes 1843200 | tf_op jit(solution)/shard_map/all_gather | solution.py:99
  13.7 74.9 %reduce-scatter.9.cloned.1.call-start = ((), (), s32[]{:S(2)}) async-start(), calls=%async_computation.9 | async-start | bytes 1843200 | tf_op jit(solution)/shard_map/reduce_scatter | solution.py:102
  14.2 8.9 %copy-start.39 = (s32[32]{0:T(128)S(1)}, s32[32]{0:T(128)}, u32[]{:S(2)}) copy-start(s32[32]{0:T(128)} %param.20) | copy-start | bytes 388
  14.2 10.3 %copy-start.27 = (bf16[2,288]{1,0:T(2,128)(2,1)S(1)}, bf16[2,288]{1,0:T(2,128)(2,1)}, u32[]{:S(2)}) copy-start(bf16[2,288]{1,0:T(2,128)(2,1)} %param.27) | copy-start | bytes 3460
  20.5 4.7 collective-permute-start
  25.4 6.2 %collective-permute-start.1 = (f32[4,6,576]{2,0,1:T(4,128)S(1)}, f32[4,6,576]{2,0,1:T(4,128)S(1)}, u32[]{:S(2)}, u32[]{:S(2)}) collective-permute-start(f32[4,6,576]{2,0,1:T(4,128)S(1)} %pad_maximum_fusion.1), channel_id=1, source_target_pairs={{0,2},{1,3},{2,0},{3,1},{4,6},{5,7},{6,4},{7,5},{8,10},{9,11},{10,... | collective-permute-start | bytes 165896 | tf_op jit(solution)/shard_map/ppermute | solution.py:25
  31.8 8.7 %copy-start.22 = (f32[4,6,2304]{2,0,1:T(4,128)}, f32[4,6,2304]{2,0,1:T(4,128)S(1)}, u32[]{:S(2)}) copy-start(f32[4,6,2304]{2,0,1:T(4,128)S(1)} %concatenate.31) | copy-start | bytes 663556
  47.4 6.5 %copy-start.16 = (bf16[640,1,288]{0,2,1:T(8,128)(2,1)}, bf16[640,1,288]{0,2,1:T(8,128)(2,1)S(1)}, u32[]{:S(2)}) copy-start(bf16[640,1,288]{0,2,1:T(8,128)(2,1)S(1)} %get-tuple-element.34) | copy-start | bytes 1105924
  47.4 6.5 %copy-start.17 = (bf16[640,1,288]{0,2,1:T(8,128)(2,1)}, bf16[640,1,288]{0,2,1:T(8,128)(2,1)S(1)}, u32[]{:S(2)}) copy-start(bf16[640,1,288]{0,2,1:T(8,128)(2,1)S(1)} %get-tuple-element.35) | copy-start | bytes 1105924
  60.5 31.3 %copy-start.29 = (bf16[1152]{0:T(1024)(128)(2,1)S(1)}, bf16[1152]{0:T(1024)(128)(2,1)}, u32[]{:S(2)}) copy-start(bf16[1152]{0:T(1024)(128)(2,1)} %param.31) | copy-start | bytes 6916
  60.5 49.4 %all-gather.10.cloned.1.call-start = ((), (), s32[]{:S(2)}) async-start(), calls=%async_computation.12 | async-start | bytes 1843200 | tf_op jit(solution)/shard_map/all_gather | solution.py:99
  63.3 67.9 %all-gather.8.cloned.1.call-start = ((), (), s32[]{:S(2)}) async-start(), calls=%async_computation.10 | async-start | bytes 1843200 | tf_op jit(solution)/shard_map/all_gather | solution.py:99
  91.6 86.2 %reduce-scatter.13.cloned.1.call-start = ((), (), s32[]{:S(2)}) async-start(), calls=%async_computation.13 | async-start | bytes 1843200 | tf_op jit(solution)/shard_map/reduce_scatter | solution.py:102
  138.9 6.1 %copy-start.12 = (bf16[640,1152]{0,1:T(8,128)(2,1)}, bf16[640,1152]{0,1:T(8,128)(2,1)S(1)}, u32[]{:S(2)}) copy-start(bf16[640,1152]{0,1:T(8,128)(2,1)S(1)} %fusion.11) | copy-start | bytes 4423684
  150.0 27.7 %copy-start.5 = (f32[640,1152]{0,1:T(8,128)S(1)}, f32[640,1152]{0,1:T(8,128)}, u32[]{:S(2)}) copy-start(f32[640,1152]{0,1:T(8,128)} %fusion.57) | copy-start | bytes 8847364
  150.0 58.3 %all-gather.12.cloned.1.call-start = ((), (), s32[]{:S(2)}) async-start(), calls=%async_computation.14 | async-start | bytes 1843200 | tf_op jit(solution)/shard_map/all_gather | solution.py:99
  188.0 50.5 %reduce-scatter.11.cloned.1.call-start = ((), (), s32[]{:S(2)}) async-start(), calls=%async_computation.11 | async-start | bytes 1843200 | tf_op jit(solution)/shard_map/reduce_scatter | solution.py:102
  188.0 6.6 %copy-start.13 = (bf16[640,1152]{0,1:T(8,128)(2,1)S(1)}, bf16[640,1152]{0,1:T(8,128)(2,1)}, u32[]{:S(2)}) copy-start(bf16[640,1152]{0,1:T(8,128)(2,1)} %copy-done.12) | copy-start | bytes 4423684
  194.6 119.1 %reduce-scatter.21.cloned.1.call-start = ((), (), s32[]{:S(2)}) async-start(), calls=%async_computation.18 | async-start | bytes 2985984 | tf_op jit(solution)/shard_map/reduce_scatter | solution.py:316
  200.1 187.1 %reduce-scatter.23.cloned.1.call-start = ((), (), s32[]{:S(2)}) async-start(), calls=%async_computation.19 | async-start | bytes 2985984 | tf_op jit(solution)/shard_map/reduce_scatter | solution.py:317
  206.0 245.6 %reduce-scatter.19.cloned.1.call-start = ((), (), s32[]{:S(2)}) async-start(), calls=%async_computation.17 | async-start | bytes 995328 | tf_op jit(solution)/shard_map/reduce_scatter | solution.py:315
  210.8 6.1 %copy-start.42 = (bf16[640,288]{0,1:T(8,128)(2,1)}, bf16[640,288]{0,1:T(8,128)(2,1)S(1)}, u32[]{:S(2)}) copy-start(bf16[640,288]{0,1:T(8,128)(2,1)S(1)} %convolution_convert_fusion.7) | copy-start | bytes 1105924
  220.9 260.0 %reduce-scatter.15.cloned.1.call-start = ((), (), s32[]{:S(2)}) async-start(), calls=%async_computation.15 | async-start | bytes 1843200 | tf_op jit(solution)/shard_map/reduce_scatter | solution.py:102
  230.3 325.7 %reduce-scatter.17.cloned.1.call-start = ((), (), s32[]{:S(2)}) async-start(), calls=%async_computation.16 | async-start | bytes 2985984 | tf_op jit(solution)/shard_map/reduce_scatter | solution.py:314
  232.5 6.0 %copy-start.7 = (f32[640,576]{0,1:T(8,128)S(1)}, f32[640,576]{0,1:T(8,128)}, u32[]{:S(2)}) copy-start(f32[640,576]{0,1:T(8,128)} %copy-done.6) | copy-start | bytes 4423684
  232.5 6.0 %copy-start.10 = (f32[640,288]{0,1:T(8,128)S(1)}, f32[640,288]{0,1:T(8,128)}, u32[]{:S(2)}) copy-start(f32[640,288]{0,1:T(8,128)} %get-tuple-element.48) | copy-start | bytes 2211844
  232.5 6.0 %copy-start.14 = (bf16[640,288]{0,1:T(8,128)(2,1)S(1)}, bf16[640,288]{0,1:T(8,128)(2,1)}, u32[]{:S(2)}) copy-start(bf16[640,288]{0,1:T(8,128)(2,1)} %reduce-scatter.9.cloned.1.call-done) | copy-start | bytes 1105924
  242.0 241.6 %copy-start.9 = (f32[640,288]{0,1:T(8,128)S(1)}, f32[640,288]{0,1:T(8,128)}, u32[]{:S(2)}) copy-start(f32[640,288]{0,1:T(8,128)} %get-tuple-element.30) | copy-start | bytes 2211844
  389.1 94.6 %copy-start.8 = (bf16[640,288]{0,1:T(8,128)(2,1)S(1)}, bf16[640,288]{0,1:T(8,128)(2,1)}, u32[]{:S(2)}) copy-start(bf16[640,288]{0,1:T(8,128)(2,1)} %reduce-scatter.13.cloned.1.call-done) | copy-start | bytes 1105924
  519.3 20.0 %copy-start.15 = (bf16[640,288]{0,1:T(8,128)(2,1)S(1)}, bf16[640,288]{0,1:T(8,128)(2,1)}, u32[]{:S(2)}) copy-start(bf16[640,288]{0,1:T(8,128)(2,1)} %reduce-scatter.15.cloned.1.call-done) | copy-start | bytes 1105924
  537.5 20.4 %copy-start.1 = (bf16[1152,1152]{1,0:T(8,128)(2,1)S(1)}, bf16[1152,1152]{1,0:T(8,128)(2,1)}, u32[]{:S(2)}) copy-start(bf16[1152,1152]{1,0:T(8,128)(2,1)} %param.30) | copy-start | bytes 7962628
  (30 other events, 100.5 us)
Sparse Core Ops, SparseCore 0:
  13.8 23.1 all-gather.5
  60.7 27.9 reduce-scatter.8
  90.8 19.0 all-gather.9
  112.0 19.0 all-gather.7
  150.2 27.5 reduce-scatter.12
  188.1 20.2 all-gather.11
  210.9 27.5 reduce-scatter.10
  242.6 71.0 reduce-scatter.20
  317.3 69.8 reduce-scatter.22
  391.4 60.0 reduce-scatter.18
  454.3 26.4 reduce-scatter.14
  484.3 71.6 reduce-scatter.16
